TPU v7x, 32 devices: a whole 2x2x4 slice. The times are simulated.
32 devices in a mesh: groups: 2 (over y), dp: 4 (over x, core), mp: 4 (over z).
Axes of the slice: x: 2, y: 2, z: 4, core: 2. Of those that a mesh axis runs over, the one named last changes fastest.
Arguments:
- base_states: bfloat16 [1280, 4096], P(('groups', 'dp'), 'mp'), parts along dimension 0, may hold values from -6 to 6
- source_states: bfloat16 [1280, 4096], P(('groups', 'dp'), 'mp'), parts along dimension 0, may hold values from -6 to 6
- source_rank: int32 [1280, 1], P(('groups', 'dp')), parts along dimension 0, may hold values from 0 to 3; in each aligned block of 160 rows (0 to 159, 160 to 319, ...) at most 80 rows name the same one
- source_row: int32 [1280], P(('groups', 'dp')), parts along dimension 0, may hold values from 0 to 159
- rotation: bfloat16 [4096, 4096], P(None, 'mp'), may hold values from -0.125 to 0.125
- mask_logits: float32 [4096], P('mp'), may hold values from -8 to 8
- norm_gain: bfloat16 [4096], replicated, may hold values from 0.25 to 1.75
- gate_weight: bfloat16 [4096, 14336], P(None, 'mp'), may hold values from -0.09375 to 0.09375
- up_weight: bfloat16 [4096, 14336], P(None, 'mp'), may hold values from -0.09375 to 0.09375
- hidden_cot: bfloat16 [1280, 14336], P(('groups', 'dp'), 'mp'), parts along dimension 0, may hold values from -0.23632812 to 0.23632812
Outputs:
- rotation_grad: float32 [8192, 4096], P(('groups', 'dp'), 'mp'), parts along dimension 0
- interchanged: bfloat16 [1280, 4096], P(('groups', 'dp'), 'mp'), parts along dimension 0
There are 2 independent parts, one for each index of `groups`. A program takes and returns all parts, laid end to end along the dimension named above; an argument that names none is the same for every part. Nothing has to cross between parts.
Inputs may be any that keep to these rules, and one draw needn't show every extreme that they name: `source_rank`: within the 160 tokens of each dp index, no dp index is named more than 80 times, and some dp index is named exactly 80 times by the tokens of some dp index.
All inputs are finite; a program needn't handle non-finite values.
Results may differ from a plain program's by a relative error of at most 0.014.
Values may be sent and summed in bfloat16 or wider, within the bound.
A program may use at most 192 MiB of HBM per device.

v0:
```python
import jax
import jax.numpy as jnp
from jax import lax
from jax.sharding import PartitionSpec as P


def contract_first(left, right):
    return lax.dot_general(
        left, right, (((0,), (0,)), ((), ())), preferred_element_type=jnp.float32
    )


def contract_last(left, right):
    return lax.dot_general(
        left, right, (((1,), (1,)), ((), ())), preferred_element_type=jnp.float32
    )


def shards(
    base_states,
    source_states,
    source_rank,
    source_row,
    rotation,
    mask_logits,
    norm_gain,
    gate_weight,
    up_weight,
    hidden_cot,
):
    tokens = base_states.shape[0]
    width = rotation.shape[0]
    ranks_of = source_rank[:, 0]
    everyone = lax.all_gather(source_states, "dp", axis=0, tiled=True)
    paired = jnp.take(everyone, ranks_of * tokens + source_row, axis=0)
    diff_local = (paired.astype(jnp.float32) - base_states.astype(jnp.float32)).astype(jnp.bfloat16)
    diff_full = lax.all_gather(diff_local, "mp", axis=1, tiled=True)
    mask = jax.nn.sigmoid(mask_logits)[None, :]
    coords = jnp.dot(diff_full, rotation, preferred_element_type=jnp.float32)
    weighted = (mask * coords).astype(jnp.bfloat16)
    moved = lax.psum_scatter(
        contract_last(rotation, weighted), "mp", scatter_dimension=0, tiled=True
    ).T
    interchanged = (base_states.astype(jnp.float32) + moved).astype(jnp.bfloat16)
    full_rows = lax.all_gather(interchanged, "mp", axis=1, tiled=True)
    states = full_rows.astype(jnp.float32)
    gain_f = norm_gain.astype(jnp.float32)[None, :]
    recip = lax.rsqrt(jnp.mean(states * states, axis=1, keepdims=True) + 1e-05)
    normed = (states * recip * gain_f).astype(jnp.bfloat16)
    gate = jnp.dot(normed, gate_weight, preferred_element_type=jnp.float32)
    up_val = jnp.dot(normed, up_weight, preferred_element_type=jnp.float32)
    sigm = jax.nn.sigmoid(gate)
    cotan = hidden_cot.astype(jnp.float32)
    dgate = (cotan * up_val * sigm * (1.0 + gate * (1.0 - sigm))).astype(jnp.bfloat16)
    dup_val = (cotan * gate * sigm).astype(jnp.bfloat16)
    partial_grad = contract_last(dgate, gate_weight) + contract_last(dup_val, up_weight)
    dnormed = lax.psum(partial_grad, "mp")
    scaled = gain_f * dnormed
    stat = jnp.sum(scaled * states, axis=1, keepdims=True)
    dinter = (recip * scaled - states * recip * recip * recip * stat / width).astype(jnp.bfloat16)
    coupled = (mask * jnp.dot(dinter, rotation, preferred_element_type=jnp.float32)).astype(
        jnp.bfloat16
    )
    rotation_grad = lax.psum_scatter(
        (contract_first(dinter, weighted) + contract_first(diff_full, coupled)).astype(
            jnp.bfloat16
        ),
        "dp",
        scatter_dimension=0,
        tiled=True,
    ).astype(jnp.float32)
    return (rotation_grad, interchanged)


def solution(mesh):
    placed = (
        P(("groups", "dp"), "mp"),
        P(("groups", "dp"), "mp"),
        P(("groups", "dp"), None),
        P(("groups", "dp")),
        P(None, "mp"),
        P("mp"),
        P(),
        P(None, "mp"),
        P(None, "mp"),
        P(("groups", "dp"), "mp"),
    )
    return jax.shard_map(
        shards,
        mesh=mesh,
        in_specs=placed,
        out_specs=(P(("groups", "dp"), "mp"), P(("groups", "dp"), "mp")),
        check_vma=False,
    )
```

profile of v0, /device:TPU:0, one launch (start us, length us, event | category | flops | bytes accessed | tf_op | source)
XLA Modules:
  0.0 437.6 jit_solution(6503187175433024214)
XLA Ops:
  7.2 0.0 copy-start.3
  7.2 0.0 copy-start.5
  7.2 0.0 all-gather.4.cloned.1.call-start
  7.2 0.7 all-gather.4.cloned.1.call-update
  7.9 0.0 all-gather.6.cloned.1.call-start
  8.0 0.7 broadcast_multiply_fusion
  8.6 0.7 compare_and_fusion
  9.3 21.2 %all-gather.4.cloned.1.call-done = bf16[640,1024]{1,0:T(8,128)(2,1)} async-done(((bf16[160,1024]{1,0:T(8,128)(2,1)}), bf16[640,1024]{1,0:T(8,128)(2,1)}) %all-gather.4.cloned.1.call-update) | async-done | bytes 1310736 | tf_op jit(solution)/shard_map/all_gather | solution.py:34
  30.5 2.7 gather_fusion
  33.2 0.0 copy-done.3
  33.2 0.9 fusion.25
  34.1 0.0 all-gather.6.cloned.1.call-update
  34.1 0.0 reduce-scatter.3.cloned.1.call-start
  34.1 0.0 copy-done.5
  34.2 32.8 %all-gather.6.cloned.1.call-done = bf16[160,4096]{1,0:T(8,128)(2,1)} async-done(((bf16[160,1024]{1,0:T(8,128)(2,1)}), bf16[160,4096]{1,0:T(8,128)(2,1)}) %all-gather.6.cloned.1.call-update) | async-done | bytes 1310736 | tf_op jit(solution)/shard_map/all_gather | solution.py:37
  66.9 5.3 %fusion.20 = bf16[160,1024]{1,0:T(8,128)(2,1)S(1)} fusion(bf16[160,4096]{1,0:T(8,128)(2,1)} %all-gather.6.cloned.1.call-done, bf16[4096,1024]{1,0:T(8,128)(2,1)} %param.14, f32[1024]{0:T(1024)S(1)} %add_divide_fusion.2), kind=kOutput, calls=%fused_computation.32 | convolution fusion | flops 1342504960 | bytes 10031104 | tf_op jit(solution)/shard_map/dot_general | solution.py:39
  72.3 7.8 %convolution_bitcast_fusion = f32[4096,160]{0,1:T(8,128)} fusion(bf16[160,1024]{1,0:T(8,128)(2,1)S(1)} %fusion.20, bf16[4096,1024]{1,0:T(8,128)(2,1)} %param.14), kind=kOutput, calls=%fused_computation.5 | convolution fusion | flops 1342177280 | bytes 11337728 | tf_op jit(solution)/shard_map/dot_general | solution.py:14
  80.1 0.0 copy-start.4
  80.1 0.0 reduce-scatter.3.cloned.1.call-update
  80.1 0.0 all-gather.8.cloned.1.call-start
  80.1 51.2 %reduce-scatter.3.cloned.1.call-done = f32[1024,160]{0,1:T(8,128)} async-done(((f32[4096,160]{0,1:T(8,128)}), f32[1024,160]{0,1:T(8,128)}) %reduce-scatter.3.cloned.1.call-update) | async-done | bytes 655376 | tf_op jit(solution)/shard_map/reduce_scatter | solution.py:41
  131.3 1.9 fusion.26
  133.2 0.0 all-gather.8.cloned.1.call-update
  133.3 0.2 all-reduce.2.cloned.1.call-start
  133.5 0.0 copy-done.4
  133.5 32.3 %all-gather.8.cloned.1.call-done = bf16[160,4096]{1,0:T(8,128)(2,1)} async-done(((bf16[160,1024]{1,0:T(8,128)(2,1)}), bf16[160,4096]{1,0:T(8,128)(2,1)}) %all-gather.8.cloned.1.call-update) | async-done | bytes 1310736 | tf_op jit(solution)/shard_map/all_gather | solution.py:45
  165.8 1.7 fusion.13
  167.5 0.0 copy-start
  167.5 0.0 copy-start.6
  167.5 16.2 %fusion.27 = f32[160,3584]{1,0:T(8,128)} fusion(bf16[4096,3584]{1,0:T(8,128)(2,1)} %param.17, bf16[160,4096]{1,0:T(8,128)(2,1)} %all-gather.8.cloned.1.call-done, f32[4096]{0:T(1024)S(1)} %convert_element_type.52, f32[160]{0:T(256)S(1)} %add_rsqrt_fusion), kind=kOutput, calls=%fused_computation.40 | convolution fusion | flops 4700241920 | bytes 32981632 | tf_op jit(solution)/shard_map/dot_general | solution.py:50
  183.7 0.0 copy-done
  183.7 0.0 copy-done.6
  183.7 25.1 %fusion.3 = f32[160,4096]{1,0:T(8,128)} fusion(bf16[4096,3584]{1,0:T(8,128)(2,1)} %param.17, bf16[4096,3584]{1,0:T(8,128)(2,1)} %param.18, bf16[160,3584]{1,0:T(8,128)(2,1)S(1)} %copy-done.6, f32[160,3584]{1,0:T(8,128)} %fusion.27, bf16[160,4096]{1,0:T(8,128)(2,1)S(1)} %copy-done, f32[4096]{0:T(1024)S(1)} %convert_element_type.52, f32[160]{0:T(256)S(1)} %add_rsqrt_fusion), kind=kOutput, calls=%fused_computation.11 | convolution fusion | flops 9404170240 | bytes 66110080 | tf_op jit(solution)/shard_map/dot_general | solution.py:14
  208.8 16.1 %convolution_add_fusion = f32[160,4096]{1,0:T(8,128)} fusion(f32[160,4096]{1,0:T(8,128)} %fusion.3, bf16[4096,3584]{1,0:T(8,128)(2,1)} %param.18, f32[160,3584]{1,0:T(8,128)} %fusion.27, bf16[160,3584]{1,0:T(8,128)(2,1)S(1)} %copy-done.6), kind=kOutput, calls=%fused_computation.6 | convolution fusion | flops 4702289920 | bytes 38043648 | tf_op jit(solution)/shard_map/dot_general | solution.py:14
  224.9 0.0 all-reduce.2.cloned.1.call-update
  224.9 0.3 reduce-scatter.5.cloned.1.call-start
  225.2 103.0 %all-reduce.2.cloned.1.call-done = f32[160,4096]{1,0:T(8,128)} async-done(((f32[160,4096]{1,0:T(8,128)}), f32[160,4096]{1,0:T(8,128)}) %all-reduce.2.cloned.1.call-update) | async-done | bytes 2621456 | tf_op jit(solution)/shard_map/psum | solution.py:57
  328.2 0.0 copy-start.1
  328.2 2.3 fusion.14
  330.5 0.2 copy-done.1
  330.7 5.3 %fusion.21 = bf16[160,1024]{1,0:T(8,128)(2,1)S(1)} fusion(bf16[4096,1024]{1,0:T(8,128)(2,1)} %param.14, f32[1024]{0:T(1024)S(1)} %add_divide_fusion.2, bf16[160,4096]{1,0:T(8,128)(2,1)S(1)} %copy-done, f32[160,4096]{1,0:T(8,128)S(1)} %copy-done.1, f32[160]{0:T(256)S(1)} %fusion.14, f32[4096]{0:T(1024)S(1)} %convert_element_type.52, f32[160]{0:T(256)S(1)} %add_rsqrt_fusion), kind=kOutput, calls=%fused_computation.33 | convolution fusion | flops 1349058560 | bytes 12670208 | tf_op jit(solution)/shard_map/dot_general | solution.py:61
  336.0 0.0 copy-start.2
  336.1 8.3 %fusion.34 = f32[4096,1024]{1,0:T(8,128)} fusion(bf16[160,1024]{1,0:T(8,128)(2,1)S(1)} %fusion.20, bf16[160,4096]{1,0:T(8,128)(2,1)S(1)} %copy-done, f32[160,4096]{1,0:T(8,128)S(1)} %copy-done.1, f32[160]{0:T(256)S(1)} %fusion.14, f32[4096]{0:T(1024)S(1)} %convert_element_type.52, f32[160]{0:T(256)S(1)} %add_rsqrt_fusion), kind=kOutput, calls=%fused_computation.49 | convolution fusion | flops 1348730880 | bytes 21054720 | tf_op jit(solution)/shard_map/dot_general | solution.py:8
  344.4 0.0 copy-done.2
  344.4 11.4 %add_convert_fusion = bf16[4096,1024]{1,0:T(8,128)(2,1)} fusion(f32[4096,1024]{1,0:T(8,128)} %fusion.34, bf16[160,4096]{1,0:T(8,128)(2,1)S(1)} %copy-done.2, bf16[160,1024]{1,0:T(8,128)(2,1)S(1)} %fusion.21), kind=kOutput, calls=%fused_computation.1 | convolution fusion | flops 1350565888 | bytes 26804224 | tf_op jit(solution)/shard_map/dot_general | solution.py:8
  355.8 0.0 reduce-scatter.5.cloned.1.call-update
  355.8 70.9 %reduce-scatter.5.cloned.1.call-done = bf16[1024,1024]{1,0:T(8,128)(2,1)} async-done(((bf16[4096,1024]{1,0:T(8,128)(2,1)}), bf16[1024,1024]{1,0:T(8,128)(2,1)}) %reduce-scatter.5.cloned.1.call-update) | async-done | bytes 2097168 | tf_op jit(solution)/shard_map/reduce_scatter | solution.py:64
  426.7 4.1 convert_element_type.60
  (4 shorter events, 0.0 us)
Async XLA Ops:
  7.2 26.0 %copy-start.3 = (bf16[160,1024]{1,0:T(8,128)(2,1)S(1)}, bf16[160,1024]{1,0:T(8,128)(2,1)}, u32[]{:S(2)}) copy-start(bf16[160,1024]{1,0:T(8,128)(2,1)} %param.10) | copy-start | bytes 983044
  7.2 27.0 %copy-start.5 = (f32[1024]{0:T(1024)S(1)}, f32[1024]{0:T(1024)}, u32[]{:S(2)}) copy-start(f32[1024]{0:T(1024)} %param.15) | copy-start | bytes 12292
  7.2 23.3 %all-gather.4.cloned.1.call-start = ((), (), s32[]{:S(2)}) async-start(), calls=%async_computation.2 | async-start | bytes 1638400 | tf_op jit(solution)/shard_map/all_gather | solution.py:34
  7.9 59.0 %all-gather.6.cloned.1.call-start = ((), (), s32[]{:S(2)}) async-start(), calls=%async_computation.3 | async-start | bytes 1638400 | tf_op jit(solution)/shard_map/all_gather | solution.py:37
  34.1 97.3 %reduce-scatter.3.cloned.1.call-start = ((), (), s32[]{:S(2)}) async-start(), calls=%async_computation.4 | async-start | bytes 3276800 | tf_op jit(solution)/shard_map/reduce_scatter | solution.py:41
  80.1 53.4 %copy-start.4 = (bf16[4096]{0:T(1024)(128)(2,1)S(1)}, bf16[4096]{0:T(1024)(128)(2,1)}, u32[]{:S(2)}) copy-start(bf16[4096]{0:T(1024)(128)(2,1)} %param.16) | copy-start | bytes 24580
  80.1 85.7 %all-gather.8.cloned.1.call-start = ((), (), s32[]{:S(2)}) async-start(), calls=%async_computation.5 | async-start | bytes 1638400 | tf_op jit(solution)/shard_map/all_gather | solution.py:45
  133.3 194.9 %all-reduce.2.cloned.1.call-start = ((), (), s32[]{:S(2)}) async-start(), calls=%async_computation.6 | async-start | bytes 5242880 | tf_op jit(solution)/shard_map/psum | solution.py:57
  167.5 16.2 %copy-start = (bf16[160,4096]{1,0:T(8,128)(2,1)S(1)}, bf16[160,4096]{1,0:T(8,128)(2,1)}, u32[]{:S(2)}) copy-start(bf16[160,4096]{1,0:T(8,128)(2,1)} %all-gather.8.cloned.1.call-done) | copy-start | bytes 3932164
  167.5 16.2 %copy-start.6 = (bf16[160,3584]{1,0:T(8,128)(2,1)S(1)}, bf16[160,3584]{1,0:T(8,128)(2,1)}, u32[]{:S(2)}) copy-start(bf16[160,3584]{1,0:T(8,128)(2,1)} %param.19) | copy-start | bytes 3440644
  224.9 201.8 %reduce-scatter.5.cloned.1.call-start = ((), (), s32[]{:S(2)}) async-start(), calls=%async_computation.7 | async-start | bytes 10485760 | tf_op jit(solution)/shard_map/reduce_scatter | solution.py:64
  328.2 2.5 copy-start.1
  336.0 8.4 %copy-start.2 = (bf16[160,4096]{1,0:T(8,128)(2,1)S(1)}, bf16[160,4096]{1,0:T(8,128)(2,1)}, u32[]{:S(2)}) copy-start(bf16[160,4096]{1,0:T(8,128)(2,1)} %all-gather.6.cloned.1.call-done) | copy-start | bytes 3932164
Sparse Core Ops, SparseCore 0:
  9.6 20.8 all-gather.3
  34.2 32.6 all-gather.5
  80.2 51.0 reduce-scatter.2
  133.4 32.3 all-gather.7
  225.0 103.0 all-reduce.1
  355.9 70.7 reduce-scatter.4
where the time goes:
time: 438 us
  waiting for transfers between devices  312 us (71%)
  matrix products  95.6 us (22%)
  between operations  14.2 us (3%)
  other arithmetic  12.2 us (3%)
    psum x1, waiting for transfers between devices, shards(): dnormed = lax.psum(partial_grad, 'mp')  103 us
    reduce_scatter x1, waiting for transfers between devices, shards(): lax.psum_scatter((contract_first(dinter, weighted) + contract_first(diff_...  70.9 us
    reduce_scatter x1, waiting for transfers between devices, shards(): lax.psum_scatter(contract_last(rotation, weighted), 'mp', scatter_dimensi...  51.2 us
    dot_general x3, matrix products, contract_last(): lax.dot_general(left, right, (((1,), (1,)), ((), ())), preferred_element_...  49 us
    all_gather x1, waiting for transfers between devices, shards(): diff_full = lax.all_gather(diff_local, 'mp', axis=1, tiled=True)  32.8 us
    all_gather x1, waiting for transfers between devices, shards(): full_rows = lax.all_gather(interchanged, 'mp', axis=1, tiled=True)  32.3 us
    all_gather x1, waiting for transfers between devices, shards(): everyone = lax.all_gather(source_states, 'dp', axis=0, tiled=True)  21.2 us
    dot_general x2, matrix products, contract_first(): lax.dot_general(left, right, (((0,), (0,)), ((), ())), preferred_element_...  19.7 us
  transfers between devices with their start and end apart: 6, of which 6 were waited for; matrix products, arithmetic and copies ran while one was open for 0% of the time, Pallas kernels for 0%

commit v1 on v0

--- a/solution.py
+++ b/solution.py
@@ -1,22 +1,530 @@
+import functools
+
 import jax
 import jax.numpy as jnp
 from jax import lax
+from jax.experimental import pallas as pl
+from jax.experimental.pallas import tpu as pltpu
 from jax.sharding import PartitionSpec as P
+
+BF = jnp.bfloat16
+F32 = jnp.float32
+CHUNKS = 2
+TILE = 256
 
 
 def contract_first(left, right):
     return lax.dot_general(
-        left, right, (((0,), (0,)), ((), ())), preferred_element_type=jnp.float32
+        left, right, (((0,), (0,)), ((), ())), preferred_element_type=F32
     )
 
 
 def contract_last(left, right):
     return lax.dot_general(
-        left, right, (((1,), (1,)), ((), ())), preferred_element_type=jnp.float32
+        left, right, (((1,), (1,)), ((), ())), preferred_element_type=F32
     )
 
 
-def shards(
+def send(src, dst, ssem, rsem, axis, dev):
+    return pltpu.make_async_remote_copy(
+        src_ref=src,
+        dst_ref=dst,
+        send_sem=ssem,
+        recv_sem=rsem,
+        device_id={axis: dev},
+        device_id_type=pl.DeviceIdType.MESH,
+    )
+
+
+def rows_of(chunk, tokens):
+    size = tokens // CHUNKS
+    return pl.ds(chunk * size, size)
+
+
+def greet(me, n, dp):
+    barrier = pltpu.get_barrier_semaphore()
+    for r in (1, 2, 3):
+        pl.semaphore_signal(
+            barrier, inc=1, device_id={"dp": partner(dp, r)}, device_id_type=pl.DeviceIdType.MESH
+        )
+
+    @pl.when(me > 0)
+    def _():
+        pl.semaphore_signal(
+            barrier, inc=1, device_id={"mp": me - 1}, device_id_type=pl.DeviceIdType.MESH
+        )
+
+    @pl.when(me < n - 1)
+    def _():
+        pl.semaphore_signal(
+            barrier, inc=1, device_id={"mp": me + 1}, device_id_type=pl.DeviceIdType.MESH
+        )
+
+    pl.semaphore_wait(barrier, 3 + jnp.minimum(me, 1) + jnp.minimum(n - 1 - me, 1))
+
+
+def partner(dp, r):
+    low = dp % 2
+    high = dp // 2
+    if r % 2:
+        low = 1 - low
+    if r // 2:
+        high = 1 - high
+    return high * 2 + low
+
+
+def line_gather(buf, ssem, rsem, me, n, tokens, use):
+    def right(k, c):
+        view = buf.at[me - k, rows_of(c, tokens)]
+        return send(view, view, ssem.at[0, k, c], rsem.at[0, k, c], "mp", me + 1)
+
+    def left(k, c):
+        view = buf.at[me + k, rows_of(c, tokens)]
+        return send(view, view, ssem.at[1, k, c], rsem.at[1, k, c], "mp", me - 1)
+
+    def arrived_right(k, c):
+        view = buf.at[me - 1 - k, rows_of(c, tokens)]
+        return send(view, view, ssem.at[0, k, c], rsem.at[0, k, c], "mp", me + 1)
+
+    def arrived_left(k, c):
+        view = buf.at[me + 1 + k, rows_of(c, tokens)]
+        return send(view, view, ssem.at[1, k, c], rsem.at[1, k, c], "mp", me - 1)
+
+    for k in range(n):
+        for c in range(CHUNKS):
+            if k > 0:
+                pl.when(me - k >= 0)(lambda: arrived_right(k - 1, c).wait_recv())
+            if k < n - 1:
+                pl.when((me - k >= 0) & (me < n - 1))(lambda: right(k, c).start())
+            if k > 0:
+                pl.when(me + k <= n - 1)(lambda: arrived_left(k - 1, c).wait_recv())
+            if k < n - 1:
+                pl.when((me + k <= n - 1) & (me > 0))(lambda: left(k, c).start())
+        if k == 0:
+            use(me)
+        else:
+            pl.when(me - k >= 0)(lambda: use(me - k))
+            pl.when(me + k <= n - 1)(lambda: use(me + k))
+    for k in range(n - 1):
+        for c in range(CHUNKS):
+            pl.when((me - k >= 0) & (me < n - 1))(lambda: right(k, c).wait_send())
+            pl.when((me + k <= n - 1) & (me > 0))(lambda: left(k, c).wait_send())
+
+
+def line_reduce(part, sums, ssem, rsem, total, me, n, tokens):
+    flip = (me * 2) // n
+    sign = 1 - 2 * flip
+    v = me + flip * (n - 1 - 2 * me)
+
+    def real(j):
+        return j + flip * (n - 1 - 2 * j)
+
+    def hop(stream, j, c):
+        way = flip if stream == 0 else 1 - flip
+        to = me + sign if stream == 0 else me - sign
+        view = sums.at[way, real(j), rows_of(c, tokens)]
+        return send(view, view, ssem.at[way, real(j), c], rsem.at[way, real(j), c], "mp", to)
+
+    def step(stream, j, c):
+        way = flip if stream == 0 else 1 - flip
+        rows = rows_of(c, tokens)
+        first = (v == 0) if stream == 0 else (v == n - 1)
+        sender = (v < j) if stream == 0 else (v > j)
+
+        @pl.when(sender & first)
+        def _():
+            sums[way, real(j), rows] = part[real(j), rows]
+
+        @pl.when(sender & jnp.logical_not(first))
+        def _():
+            hop(stream, j, c).wait_recv()
+            sums[way, real(j), rows] = (
+                sums[way, real(j), rows].astype(F32) + part[real(j), rows].astype(F32)
+            ).astype(BF)
+
+        pl.when(sender)(lambda: hop(stream, j, c).start())
+
+    for s in range(n - 1):
+        for stream, j in ((0, n - 1 - s), (1, s)):
+            for c in range(CHUNKS):
+                step(stream, j, c)
+    total[...] = part[me].astype(F32)
+    for way, there, frm in ((0, me > 0, me - 1), (1, me < n - 1, me + 1)):
+
+        @pl.when(there)
+        def _():
+            for c in range(CHUNKS):
+                view = sums.at[way, me, rows_of(c, tokens)]
+                send(view, view, ssem.at[way, me, c], rsem.at[way, me, c], "mp", frm).wait_recv()
+            total[...] += sums[way, me].astype(F32)
+
+    for s in range(n - 1):
+        for stream, j in ((0, n - 1 - s), (1, s)):
+            sender = (v < j) if stream == 0 else (v > j)
+            for c in range(CHUNKS):
+                pl.when(sender)(lambda: hop(stream, j, c).wait_send())
+
+
+def times_rotation(left, rot, block, acc):
+    shard = left.shape[1]
+
+    def body(i, carry):
+        cols = pl.ds(pl.multiple_of(i * TILE, TILE), TILE)
+        rows = pl.ds(pl.multiple_of(block * shard, shard), shard)
+        acc[:, cols] += jnp.dot(left, rot[rows, cols], preferred_element_type=F32)
+        return carry
+
+    lax.fori_loop(0, acc.shape[1] // TILE, body, 0)
+
+
+def front_kernel(
+    n,
+    src,
+    base,
+    index,
+    logits,
+    rot_hbm,
+    weighted,
+    diff_full,
+    inter_full,
+    inter_own,
+    rot,
+    pool,
+    part,
+    sums,
+    acc,
+    rot_sem,
+    pool_s,
+    pool_r,
+    gd_s,
+    gd_r,
+    red_s,
+    red_r,
+    gi_s,
+    gi_r,
+):
+    me = lax.axis_index("mp")
+    dp = lax.axis_index("dp")
+    tokens, width = src.shape
+    load = pltpu.make_async_copy(rot_hbm, rot, rot_sem)
+    load.start()
+    greet(me, n, dp)
+
+    def across(i, frm, to):
+        return send(frm, pool.at[to[0]], pool_s.at[i], pool_r.at[i], "dp", to[1])
+
+    near, far, both = partner(dp, 1), partner(dp, 2), partner(dp, 3)
+    one = across(0, src, (2, far))
+    two = across(1, src, (1, near))
+    one.start()
+    two.start()
+    pool[0] = src[...]
+    one.wait_recv()
+    three = across(2, pool.at[2], (3, near))
+    three.start()
+    owner = index[...]
+    lane = lax.broadcasted_iota(jnp.int32, (tokens, tokens), 1)
+
+    def pick(slot, who):
+        hit = (owner == lane + who * tokens).astype(F32).astype(BF)
+        return jnp.dot(hit, pool[slot], preferred_element_type=F32)
+
+    acc[...] = pick(0, dp) + pick(2, far)
+    two.wait_recv()
+    acc[...] += pick(1, near)
+    three.wait_recv()
+    acc[...] += pick(3, both)
+    diff_full[me] = (acc[...] - base[...].astype(F32)).astype(BF)
+    acc[...] = jnp.zeros_like(acc)
+
+    first = [True]
+
+    def use(j):
+        if first[0]:
+            first[0] = False
+            load.wait()
+        times_rotation(diff_full[j], rot, j, acc)
+
+    line_gather(diff_full, gd_s, gd_r, me, n, tokens, use)
+    weighted[...] = (jax.nn.sigmoid(logits[...]) * acc[...]).astype(BF)
+
+    def back(i, carry):
+        per = width // TILE
+        rows = pl.ds(pl.multiple_of(i * TILE, TILE), TILE)
+        cols = pl.ds(pl.multiple_of((i % per) * TILE, TILE), TILE)
+        part[i // per, :, cols] = contract_last(weighted[...], rot[rows, :]).astype(BF)
+        return carry
+
+    lax.fori_loop(0, rot.shape[0] // TILE, back, 0)
+    line_reduce(part, sums, red_s, red_r, acc, me, n, tokens)
+    mine = (base[...].astype(F32) + acc[...]).astype(BF)
+    inter_full[me] = mine
+    inter_own[...] = mine
+    line_gather(inter_full, gi_s, gi_r, me, n, tokens, lambda j: None)
+    one.wait_send()
+    two.wait_send()
+    three.wait_send()
+
+
+def recip_of(inter, n):
+    tokens, width = inter.shape[1:]
+    square = jnp.zeros((tokens, 1), F32)
+    for j in range(n):
+        block = inter[j].astype(F32)
+        square = square + jnp.sum(block * block, axis=1, keepdims=True)
+    return lax.rsqrt(square / (n * width) + 1e-05)
+
+
+def ffn_kernel(n, inter, gain, wg, wu, cot, out, normed, total):
+    tokens, width = inter.shape[1:]
+    step = pl.program_id(0)
+
+    @pl.when(step == 0)
+    def _():
+        recip = recip_of(inter, n)
+        for j in range(n):
+            cols = pl.ds(j * width, width)
+            scale = gain[:, cols].astype(F32)
+            normed[:, cols] = (inter[j].astype(F32) * recip * scale).astype(BF)
+        total[...] = jnp.zeros_like(total)
+
+    gate = jnp.dot(normed[...], wg[...], preferred_element_type=F32)
+    up = jnp.dot(normed[...], wu[...], preferred_element_type=F32)
+    sig = jax.nn.sigmoid(gate)
+    cotan = cot[...].astype(F32)
+    dgate = (cotan * up * sig * (1.0 + gate * (1.0 - sig))).astype(BF)
+    dup = (cotan * gate * sig).astype(BF)
+    for i in range(n * width // 512):
+        rows = pl.ds(i * 512, 512)
+        total[:, rows] += contract_last(dgate, wg[rows, :]) + contract_last(dup, wu[rows, :])
+
+    @pl.when(step == pl.num_programs(0) - 1)
+    def _():
+        for j in range(n):
+            out[j] = total[:, pl.ds(j * width, width)].astype(BF)
+
+
+def back_kernel(
+    n,
+    part,
+    inter,
+    gain,
+    logits,
+    rot_hbm,
+    dinter_all,
+    coupled_all,
+    rot,
+    sums,
+    dn,
+    dinter,
+    acc,
+    stat,
+    rot_sem,
+    red_s,
+    red_r,
+    ga_s,
+    ga_r,
+    ex_s,
+    ex_r,
+    co_s,
+    co_r,
+):
+    me = lax.axis_index("mp")
+    dp = lax.axis_index("dp")
+    tokens, width = part.shape[1:]
+    load = pltpu.make_async_copy(rot_hbm, rot, rot_sem)
+    load.start()
+    greet(me, n, dp)
+    line_reduce(part, sums, red_s, red_r, acc, me, n, tokens)
+    dn[me] = acc[...].astype(BF)
+    stat[...] = jnp.zeros_like(stat)
+
+    def use(j):
+        scaled = gain[j].astype(F32) * dn[j].astype(F32)
+        stat[...] += jnp.sum(scaled * inter[j].astype(F32), axis=1, keepdims=True)
+
+    line_gather(dn, ga_s, ga_r, me, n, tokens, use)
+    recip = recip_of(inter, n)
+    coef = recip * recip * recip * stat[...] / (n * width)
+
+    copies = []
+    for j in range(n):
+        scaled = gain[j].astype(F32) * dn[j].astype(F32)
+        dinter[j] = (recip * scaled - inter[j].astype(F32) * coef).astype(BF)
+    for r in (2, 3, 1):
+        to = partner(dp, r)
+        copy = send(dinter.at[to], dinter_all.at[r], ex_s.at[r], ex_r.at[r], "dp", to)
+        copy.start()
+        copies.append(copy)
+    dinter_all[0] = dinter[dp]
+    load.wait()
+    acc[...] = jnp.zeros_like(acc)
+    for j in range(n):
+        times_rotation(dinter[j], rot, j, acc)
+    coupled_all[0] = (jax.nn.sigmoid(logits[...]) * acc[...]).astype(BF)
+    near, far = partner(dp, 1), partner(dp, 2)
+    own = coupled_all.at[0]
+    one = send(own, coupled_all.at[2], co_s.at[0], co_r.at[0], "dp", far)
+    two = send(own, coupled_all.at[1], co_s.at[1], co_r.at[1], "dp", near)
+    one.start()
+    two.start()
+    one.wait_recv()
+    three = send(coupled_all.at[2], coupled_all.at[3], co_s.at[2], co_r.at[2], "dp", near)
+    three.start()
+    for copy in copies:
+        copy.wait_recv()
+    two.wait_recv()
+    three.wait_recv()
+    for copy in copies + [one, two, three]:
+        copy.wait_send()
+
+
+def grad_kernel(count, *refs):
+    dinter, coupled = refs[0], refs[1]
+    weighted = refs[2 : 2 + count]
+    diff = refs[2 + count : 2 + 2 * count]
+    out = refs[-1]
+    rows = pl.program_id(0)
+    acc = jnp.zeros(out.shape, F32)
+    for r in range(count):
+        acc = acc + contract_first(dinter[r], weighted[r][...])
+        acc = acc + contract_first(diff[r][...], coupled[r])
+    out[...] = acc
+
+
+def vmem():
+    return pl.BlockSpec(memory_space=pltpu.VMEM)
+
+
+def anywhere():
+    return pl.BlockSpec(memory_space=pl.ANY)
+
+
+def dma(*shape):
+    return pltpu.SemaphoreType.DMA(shape)
+
+
+def fast(
+    n,
+    base_states,
+    source_states,
+    source_rank,
+    source_row,
+    rotation,
+    mask_logits,
+    norm_gain,
+    gate_weight,
+    up_weight,
+    hidden_cot,
+):
+    tokens, width = base_states.shape
+    hidden = gate_weight.shape[1]
+    full = rotation.shape[0]
+    peers = 4
+    index = source_rank * tokens + source_row[:, None]
+    logits = mask_logits[None, :]
+    whole = jax.ShapeDtypeStruct((n, tokens, width), BF)
+    one = jax.ShapeDtypeStruct((tokens, width), BF)
+    line = (2, n - 1, CHUNKS)
+    weighted, diff_full, inter_full, interchanged = pl.pallas_call(
+        functools.partial(front_kernel, n),
+        out_shape=(one, whole, whole, one),
+        in_specs=[vmem()] * 4 + [anywhere()],
+        out_specs=(vmem(),) * 4,
+        scratch_shapes=[
+            pltpu.VMEM((full, width), BF),
+            pltpu.VMEM((peers, tokens, width), BF),
+            pltpu.VMEM((n, tokens, width), BF),
+            pltpu.VMEM((2, n, tokens, width), BF),
+            pltpu.VMEM((tokens, width), F32),
+            pltpu.SemaphoreType.DMA,
+            dma(3),
+            dma(3),
+            dma(*line),
+            dma(*line),
+            dma(2, n, CHUNKS),
+            dma(2, n, CHUNKS),
+            dma(*line),
+            dma(*line),
+        ],
+        compiler_params=pltpu.CompilerParams(collective_id=0, has_side_effects=True),
+        name="front",
+    )(source_states, base_states, index, logits, rotation)
+
+    dp = lax.axis_index("dp")
+    weights_of = [weighted]
+    diffs_of = [diff_full[dp]]
+    for r in range(1, peers):
+        perm = [(i, i ^ r) for i in range(peers)]
+        weights_of.append(lax.ppermute(weighted, "dp", perm))
+        diffs_of.append(lax.ppermute(diff_full[dp ^ r], "dp", perm))
+
+    block = 512 if hidden % 512 == 0 else hidden
+    part = pl.pallas_call(
+        functools.partial(ffn_kernel, n),
+        out_shape=whole,
+        grid=(hidden // block,),
+        in_specs=[
+            pl.BlockSpec((n, tokens, width), lambda i: (0, 0, 0)),
+            pl.BlockSpec((1, full), lambda i: (0, 0)),
+            pl.BlockSpec((full, block), lambda i: (0, i)),
+            pl.BlockSpec((full, block), lambda i: (0, i)),
+            pl.BlockSpec((tokens, block), lambda i: (0, i)),
+        ],
+        out_specs=pl.BlockSpec((n, tokens, width), lambda i: (0, 0, 0)),
+        scratch_shapes=[pltpu.VMEM((tokens, full), BF), pltpu.VMEM((tokens, full), F32)],
+        cost_estimate=pl.CostEstimate(
+            flops=8 * tokens * full * hidden,
+            bytes_accessed=4 * full * hidden,
+            transcendentals=tokens * hidden,
+        ),
+        name="ffn",
+    )(inter_full, norm_gain[None, :], gate_weight, up_weight, hidden_cot)
+
+    dinter_all, coupled_all = pl.pallas_call(
+        functools.partial(back_kernel, n),
+        out_shape=(jax.ShapeDtypeStruct((peers, tokens, width), BF),) * 2,
+        in_specs=[vmem()] * 4 + [anywhere()],
+        out_specs=(vmem(),) * 2,
+        scratch_shapes=[
+            pltpu.VMEM((full, width), BF),
+            pltpu.VMEM((2, n, tokens, width), BF),
+            pltpu.VMEM((n, tokens, width), BF),
+            pltpu.VMEM((n, tokens, width), BF),
+            pltpu.VMEM((tokens, width), F32),
+            pltpu.VMEM((tokens, 1), F32),
+            pltpu.SemaphoreType.DMA,
+            dma(2, n, CHUNKS),
+            dma(2, n, CHUNKS),
+            dma(*line),
+            dma(*line),
+            dma(peers),
+            dma(peers),
+            dma(3),
+            dma(3),
+        ],
+        compiler_params=pltpu.CompilerParams(collective_id=1, has_side_effects=True),
+        name="back",
+    )(part, inter_full, norm_gain.reshape(n, 1, width), logits, rotation)
+
+    rows = 256
+    rotation_grad = pl.pallas_call(
+        functools.partial(grad_kernel, peers),
+        out_shape=jax.ShapeDtypeStruct((full // peers, width), F32),
+        grid=(full // peers // rows,),
+        in_specs=[
+            pl.BlockSpec((peers, tokens, rows), lambda i: (0, 0, i)),
+            pl.BlockSpec((peers, tokens, width), lambda i: (0, 0, 0)),
+        ]
+        + [pl.BlockSpec((tokens, width), lambda i: (0, 0))] * peers
+        + [pl.BlockSpec((tokens, rows), lambda i: (0, i))] * peers,
+        out_specs=pl.BlockSpec((rows, width), lambda i: (i, 0)),
+        name="grad",
+    )(dinter_all, coupled_all, *weights_of, *diffs_of)
+    return (rotation_grad, interchanged)
+
+
+def plain(
     base_states,
     source_states,
     source_rank,
@@ -73,6 +581,24 @@
 
 
 def solution(mesh):
+    n = mesh.shape["mp"]
+
+    def shards(*args):
+        width = args[0].shape[1]
+        tokens = args[0].shape[0]
+        full = args[4].shape[0]
+        fits = (
+            width % TILE == 0
+            and mesh.shape["dp"] == 4
+            and 1 < n <= 8
+            and n * width == full
+            and full // 4 == width
+            and tokens % (16 * CHUNKS) == 0
+        )
+        if fits:
+            return fast(n, *args)
+        return plain(*args)
+
     placed = (
         P(("groups", "dp"), "mp"),
         P(("groups", "dp"), "mp"),

time: 438 us -> 230 us (0.53)
  waiting for transfers between devices: 312 us -> 5.62 us
  Pallas kernels: 0 us -> 213 us
  matrix products: 95.6 us -> 0 us
  between operations: 14.2 us -> 0.77 us
  other arithmetic: 12.2 us -> 0.7 us
    pallas_call x0 -> x4, Pallas kernels: none -> 213 us  [the longest x1 92.3 us: fast(): pl.pallas_call(functools.partial(front_kernel, n), out_shape=(one, whole,...]
    reduce_scatter x2 -> x0, waiting for transfers between devices: 122 us -> none  [the longest x1 70.9 us: shards(): lax.psum_scatter((contract_first(dinter, weighted) + contract_first(diff_...]
    psum x1 -> x0, waiting for transfers between devices: 103 us -> none  [shards(): dnormed = lax.psum(partial_grad, 'mp')]
    dot_general x8 -> x0, matrix products: 95.6 us -> none  [the longest x3 49 us: contract_last(): lax.dot_general(left, right, (((1,), (1,)), ((), ())), preferred_element_...]
    all_gather x3 -> x0, waiting for transfers between devices: 86.2 us -> none  [the longest x1 32.8 us: shards(): diff_full = lax.all_gather(diff_local, 'mp', axis=1, tiled=True)]
    convert_element_type x4 -> x0, other arithmetic: 6.86 us -> none  [the longest x1 4.07 us: shards(): rotation_grad = lax.psum_scatter((contract_first(dinter, weighted) + cont...]
    ppermute x0 -> x6, waiting for transfers between devices: none -> 5.62 us  [the longest x3 5.62 us: fast(): diffs_of.append(lax.ppermute(diff_full[dp ^ r], 'dp', perm))]
  transfers between devices with their start and end apart: 6 -> 6, of which waited for: 6 -> 1; matrix products, arithmetic and copies ran while one was open for 0% -> 1% of each run, Pallas kernels for 0% -> 49%
where the time goes in v1:
time: 230 us
  Pallas kernels  213 us (93%)
  local copies, waits for them, and re-layouts  5.96 us (3%)
  waiting for transfers between devices  5.62 us (2%)
  starting transfers between devices  3.78 us (2%)
    pallas_call x1, Pallas kernels, fast(): pl.pallas_call(functools.partial(front_kernel, n), out_shape=(one, whole,...  92.3 us
    pallas_call x1, Pallas kernels, fast(): pl.pallas_call(functools.partial(back_kernel, n), out_shape=(jax.ShapeDty...  75 us
    pallas_call x1, Pallas kernels, fast(): pl.pallas_call(functools.partial(ffn_kernel, n), out_shape=whole, grid=(h...  37.3 us
    pallas_call x1, Pallas kernels, fast(): pl.pallas_call(functools.partial(grad_kernel, peers), out_shape=jax.Shape...  8.39 us
    ppermute x3, waiting for transfers between devices, fast(): diffs_of.append(lax.ppermute(diff_full[dp ^ r], 'dp', perm))  5.62 us
  transfers between devices with their start and end apart: 6, of which 1 were waited for; matrix products, arithmetic and copies ran while one was open for 1% of the time, Pallas kernels for 49%

profile of v1, /device:TPU:0, one launch (start us, length us, event | category | flops | bytes accessed | tf_op | source)
XLA Modules:
  0.0 229.9 jit_solution(16760449632613353151)
XLA Ops:
  0.6 0.7 multiply_add_fusion
  1.3 0.8 copy.18.index
  2.1 92.3 %front.1 = (bf16[160,1024]{1,0:T(8,128)(2,1)}, bf16[4,160,1024]{2,1,0:T(8,128)(2,1)}, bf16[4,160,1024]{2,1,0:T(8,128)(2,1)}, bf16[160,1024]{1,0:T(8,128)(2,1)}) custom-call(bf16[160,1024]{1,0:T(8,128)(2,1)} %src.1, bf16[160,1024]{1,0:T(8,128)(2,1)} %base.1, s32[160,1]{1,0:T(8,128)} %copy.18.index, f32[1,1024]{1,0:T(1,128)} %bitcast.10, ...), custom_call_target="tpu_custom_call" | custom-call | tf_op jit(solution)/shard_map/front/pallas_call | solution.py:429
  94.5 0.0 copy-start
  94.5 0.0 copy-start.8
  94.5 2.2 dynamic-slice_bitcast_fusion
  96.6 0.0 collective-permute-start.5
  96.6 0.0 copy-done
  96.6 1.7 collective-permute-start.2
  98.4 1.1 collective-permute-start.1
  99.5 0.0 collective-permute-start
  99.5 0.9 collective-permute-start.4
  100.4 0.0 copy-done.8
  100.4 0.6 broadcast_in_dim.11.gain
  101.0 5.6 %collective-permute-done.5.refs_9_ = bf16[160,1024]{1,0:T(8,128)(2,1)S(1)} collective-permute-done((bf16[160,1024]{1,0:T(8,128)(2,1)S(1)}, bf16[160,1024]{1,0:T(8,128)(2,1)S(1)}, u32[]{:S(2)}, u32[]{:S(2)}) %collective-permute-start.5) | collective-permute-done | bytes 327712 | tf_op jit(solution)/shard_map/ppermute | solution.py:460
  106.7 0.0 copy-start.1
  106.7 0.0 collective-permute-start.3
  106.7 37.3 %ffn.1.part = bf16[4,160,1024]{2,1,0:T(8,128)(2,1)} custom-call(bf16[4,160,1024]{2,1,0:T(8,128)(2,1)} %get-tuple-element.8.inter, bf16[1,4096]{1,0:T(2,128)(2,1)} %broadcast_in_dim.11.gain, bf16[4096,3584]{1,0:T(8,128)(2,1)} %wg.1, bf16[4096,3584]{1,0:T(8,128)(2,1)} %wu.1, bf16[160,3584]{1,0:T(8,128)(2,1)} %cot.1), custom_call_target="tpu_custom_call" | custom-call | flops 18790481920 | bytes 58720256 | tf_op jit(solution)/shard_map/ffn/pallas_call | solution.py:463
  144.0 0.0 copy-done.1
  144.0 0.6 reshape.8.gain
  144.6 75.0 %back.1 = (bf16[4,160,1024]{2,1,0:T(8,128)(2,1)}, bf16[4,160,1024]{2,1,0:T(8,128)(2,1)}) custom-call(bf16[4,160,1024]{2,1,0:T(8,128)(2,1)} %ffn.1.part, bf16[4,160,1024]{2,1,0:T(8,128)(2,1)} %get-tuple-element.8.inter, bf16[4,1,1024]{2,1,0:T(2,128)(2,1)} %reshape.8.gain, f32[1,1024]{1,0:T(1,128)} %bitcast.11, bf16[4096,1024]{1,0:T(8,128)(2,1)} %rot_hbm.3), custom_call_target="tpu_custom_call" | custom-call | tf_op jit(solution)/shard_map/back/pallas_call | solution.py:484
  219.6 0.0 collective-permute-done.4.refs_8_
  219.6 0.0 copy-start.5
  219.6 0.0 collective-permute-done.3.refs_7_
  219.6 0.0 copy-start.6
  219.6 0.0 collective-permute-done.2.refs_5_
  219.6 0.0 copy-start.2
  219.7 0.0 collective-permute-done.1.refs_4_
  219.7 0.0 copy-start.3
  219.7 0.0 collective-permute-done.refs_3_
  219.7 0.0 copy-start.4
  219.7 0.6 copy-done.5
  220.3 0.1 copy-done.6
  220.5 0.1 copy-done.2
  220.6 0.1 copy-done.3
  220.7 0.1 copy-done.4
  220.8 0.0 copy-start.7
  220.8 8.4 %grad.1 = f32[1024,1024]{1,0:T(8,128)} custom-call(bf16[4,160,1024]{2,1,0:T(8,128)(2,1)} %get-tuple-element.9.refs_0_, bf16[4,160,1024]{2,1,0:T(8,128)(2,1)} %get-tuple-element.10.refs_1_, bf16[160,1024]{1,0:T(8,128)(2,1)} %get-tuple-element.11.refs_2_, bf16[160,1024]{1,0:T(8,128)(2,1)} %copy-done.4, bf16[160,1024]{1,0:T(8,128)(2,1)} %copy-done.3, ...), custom_call_target="tpu_custom_call" | custom-call | tf_op jit(solution)/shard_map/grad/pallas_call | solution.py:511
  229.1 0.0 copy-done.7
  229.2 0.7 copy.21
Async XLA Ops:
  94.5 2.2 copy-start
  94.5 6.0 %copy-start.8 = (bf16[4096]{0:T(1024)(128)(2,1)S(1)}, bf16[4096]{0:T(1024)(128)(2,1)}, u32[]{:S(2)}) copy-start(bf16[4096]{0:T(1024)(128)(2,1)} %param.16) | copy-start | bytes 24580
  96.6 10.0 %collective-permute-start.5 = (bf16[160,1024]{1,0:T(8,128)(2,1)S(1)}, bf16[160,1024]{1,0:T(8,128)(2,1)S(1)}, u32[]{:S(2)}, u32[]{:S(2)}) collective-permute-start(bf16[160,1024]{1,0:T(8,128)(2,1)S(1)} %get-tuple-element.14), channel_id=1, source_target_pairs={{0,12},{4,8},{8,4},{12,0},{1,13},{5,9},{9,5},{13,1},{2,14},{6,10},... | collective-permute-start | bytes 983048 | tf_op jit(solution)/shard_map/ppermute | solution.py:460
  96.6 123.0 %collective-permute-start.2 = (bf16[160,1024]{1,0:T(8,128)(2,1)S(1)}, bf16[160,1024]{1,0:T(8,128)(2,1)S(1)}, u32[]{:S(2)}, u32[]{:S(2)}) collective-permute-start(bf16[160,1024]{1,0:T(8,128)(2,1)S(1)} %copy-done), channel_id=1, source_target_pairs={{0,12},{4,8},{8,4},{12,0},{1,13},{5,9},{9,5},{13,1},{2,14},{6,10},... | collective-permute-start | bytes 983048 | tf_op jit(solution)/shard_map/ppermute | solution.py:459
  98.4 121.3 %collective-permute-start.1 = (bf16[160,1024]{1,0:T(8,128)(2,1)S(1)}, bf16[160,1024]{1,0:T(8,128)(2,1)S(1)}, u32[]{:S(2)}, u32[]{:S(2)}) collective-permute-start(bf16[160,1024]{1,0:T(8,128)(2,1)S(1)} %copy-done), channel_id=1, source_target_pairs={{0,8},{4,12},{8,0},{12,4},{1,9},{5,13},{9,1},{13,5},{2,10},{6,14},... | collective-permute-start | bytes 983048 | tf_op jit(solution)/shard_map/ppermute | solution.py:459
  99.5 120.2 %collective-permute-start = (bf16[160,1024]{1,0:T(8,128)(2,1)S(1)}, bf16[160,1024]{1,0:T(8,128)(2,1)S(1)}, u32[]{:S(2)}, u32[]{:S(2)}) collective-permute-start(bf16[160,1024]{1,0:T(8,128)(2,1)S(1)} %copy-done), channel_id=1, source_target_pairs={{0,4},{4,0},{8,12},{12,8},{1,5},{5,1},{9,13},{13,9},{2,6},{6,2},{1... | collective-permute-start | bytes 983048 | tf_op jit(solution)/shard_map/ppermute | solution.py:459
  99.5 120.1 %collective-permute-start.4 = (bf16[160,1024]{1,0:T(8,128)(2,1)S(1)}, bf16[160,1024]{1,0:T(8,128)(2,1)S(1)}, u32[]{:S(2)}, u32[]{:S(2)}) collective-permute-start(bf16[160,1024]{1,0:T(8,128)(2,1)S(1)} %get-tuple-element.15), channel_id=1, source_target_pairs={{0,8},{4,12},{8,0},{12,4},{1,9},{5,13},{9,1},{13,5},{2,10},{6,14},... | collective-permute-start | bytes 983048 | tf_op jit(solution)/shard_map/ppermute | solution.py:460
  106.7 37.3 %copy-start.1 = (bf16[160,1024]{1,0:T(8,128)(2,1)}, bf16[160,1024]{1,0:T(8,128)(2,1)S(1)}, u32[]{:S(2)}) copy-start(bf16[160,1024]{1,0:T(8,128)(2,1)S(1)} %collective-permute-done.5.refs_9_) | copy-start | bytes 983044
  106.7 113.0 %collective-permute-start.3 = (bf16[160,1024]{1,0:T(8,128)(2,1)S(1)}, bf16[160,1024]{1,0:T(8,128)(2,1)S(1)}, u32[]{:S(2)}, u32[]{:S(2)}) collective-permute-start(bf16[160,1024]{1,0:T(8,128)(2,1)S(1)} %get-tuple-element.16), channel_id=1, source_target_pairs={{0,4},{4,0},{8,12},{12,8},{1,5},{5,1},{9,13},{13,9},{2,6},{6,2},{1... | collective-permute-start | bytes 983048 | tf_op jit(solution)/shard_map/ppermute | solution.py:460
  219.6 0.7 copy-start.5
  219.6 0.8 copy-start.6
  219.6 0.9 copy-start.2
  219.7 1.0 copy-start.3
  219.7 1.1 copy-start.4
  220.8 8.4 %copy-start.7 = (bf16[160,1024]{1,0:T(8,128)(2,1)S(1)}, bf16[160,1024]{1,0:T(8,128)(2,1)}, u32[]{:S(2)}) copy-start(bf16[160,1024]{1,0:T(8,128)(2,1)} %get-tuple-element.21) | copy-start | bytes 983044

commit v2 on v1

--- a/solution.py
+++ b/solution.py
@@ -10,7 +10,7 @@
 BF = jnp.bfloat16
 F32 = jnp.float32
 CHUNKS = 2
-TILE = 256
+TILE = 512
 
 
 def contract_first(left, right):
@@ -74,44 +74,44 @@
 
 
 def line_gather(buf, ssem, rsem, me, n, tokens, use):
-    def right(k, c):
-        view = buf.at[me - k, rows_of(c, tokens)]
-        return send(view, view, ssem.at[0, k, c], rsem.at[0, k, c], "mp", me + 1)
-
-    def left(k, c):
-        view = buf.at[me + k, rows_of(c, tokens)]
-        return send(view, view, ssem.at[1, k, c], rsem.at[1, k, c], "mp", me - 1)
-
-    def arrived_right(k, c):
-        view = buf.at[me - 1 - k, rows_of(c, tokens)]
-        return send(view, view, ssem.at[0, k, c], rsem.at[0, k, c], "mp", me + 1)
-
-    def arrived_left(k, c):
-        view = buf.at[me + 1 + k, rows_of(c, tokens)]
-        return send(view, view, ssem.at[1, k, c], rsem.at[1, k, c], "mp", me - 1)
-
-    for k in range(n):
-        for c in range(CHUNKS):
+    def hop(way, k, c):
+        shard, to = (me - k, me + 1) if way == 0 else (me + k, me - 1)
+        view = buf.at[shard, rows_of(c, tokens)]
+        return send(view, view, ssem.at[way, k, c], rsem.at[way, k, c], "mp", to)
+
+    def arrival(way, k, c):
+        shard, frm = (me - 1 - k, me - 1) if way == 0 else (me + 1 + k, me + 1)
+        view = buf.at[shard, rows_of(c, tokens)]
+        return send(view, view, ssem.at[way, k, c], rsem.at[way, k, c], "mp", frm)
+
+    def sends(way, k):
+        if way == 0:
+            return (me - k >= 0) & (me < n - 1)
+        return (me + k <= n - 1) & (me > 0)
+
+    def step(c, k):
+        here = (me - k >= 0, me + k <= n - 1)
+        for way in (0, 1):
             if k > 0:
-                pl.when(me - k >= 0)(lambda: arrived_right(k - 1, c).wait_recv())
+                pl.when(here[way])(lambda: arrival(way, k - 1, c).wait_recv())
             if k < n - 1:
-                pl.when((me - k >= 0) & (me < n - 1))(lambda: right(k, c).start())
-            if k > 0:
-                pl.when(me + k <= n - 1)(lambda: arrived_left(k - 1, c).wait_recv())
-            if k < n - 1:
-                pl.when((me + k <= n - 1) & (me > 0))(lambda: left(k, c).start())
+                pl.when(sends(way, k))(lambda: hop(way, k, c).start())
         if k == 0:
-            use(me)
+            use(c, me)
         else:
-            pl.when(me - k >= 0)(lambda: use(me - k))
-            pl.when(me + k <= n - 1)(lambda: use(me + k))
-    for k in range(n - 1):
-        for c in range(CHUNKS):
-            pl.when((me - k >= 0) & (me < n - 1))(lambda: right(k, c).wait_send())
-            pl.when((me + k <= n - 1) & (me > 0))(lambda: left(k, c).wait_send())
-
-
-def line_reduce(part, sums, ssem, rsem, total, me, n, tokens):
+            pl.when(here[0])(lambda: use(c, me - k))
+            pl.when(here[1])(lambda: use(c, me + k))
+
+    def drain():
+        for k in range(n - 1):
+            for c in range(CHUNKS):
+                for way in (0, 1):
+                    pl.when(sends(way, k))(lambda: hop(way, k, c).wait_send())
+
+    return step, drain
+
+
+def line_reduce(part, sums, ssem, rsem, total, me, n, tokens, prepare):
     flip = (me * 2) // n
     sign = 1 - 2 * flip
     v = me + flip * (n - 1 - 2 * me)
@@ -125,7 +125,7 @@
         view = sums.at[way, real(j), rows_of(c, tokens)]
         return send(view, view, ssem.at[way, real(j), c], rsem.at[way, real(j), c], "mp", to)
 
-    def step(stream, j, c):
+    def one(stream, j, c):
         way = flip if stream == 0 else 1 - flip
         rows = rows_of(c, tokens)
         first = (v == 0) if stream == 0 else (v == n - 1)
@@ -144,34 +144,40 @@
 
         pl.when(sender)(lambda: hop(stream, j, c).start())
 
-    for s in range(n - 1):
+    def step(c, s):
         for stream, j in ((0, n - 1 - s), (1, s)):
-            for c in range(CHUNKS):
-                step(stream, j, c)
-    total[...] = part[me].astype(F32)
-    for way, there, frm in ((0, me > 0, me - 1), (1, me < n - 1, me + 1)):
-
-        @pl.when(there)
-        def _():
-            for c in range(CHUNKS):
-                view = sums.at[way, me, rows_of(c, tokens)]
+            if prepare is not None and s <= n - 1 - s and (stream == 0 or s < n - 1 - s):
+                prepare(c, real(j))
+            one(stream, j, c)
+
+    def finish(c):
+        rows = rows_of(c, tokens)
+        total[rows] = part[me, rows].astype(F32)
+        for way, there, frm in ((0, me > 0, me - 1), (1, me < n - 1, me + 1)):
+
+            @pl.when(there)
+            def _():
+                view = sums.at[way, me, rows]
                 send(view, view, ssem.at[way, me, c], rsem.at[way, me, c], "mp", frm).wait_recv()
-            total[...] += sums[way, me].astype(F32)
-
-    for s in range(n - 1):
-        for stream, j in ((0, n - 1 - s), (1, s)):
-            sender = (v < j) if stream == 0 else (v > j)
-            for c in range(CHUNKS):
-                pl.when(sender)(lambda: hop(stream, j, c).wait_send())
-
-
-def times_rotation(left, rot, block, acc):
+                total[rows] += sums[way, me, rows].astype(F32)
+
+    def drain():
+        for s in range(n - 1):
+            for stream, j in ((0, n - 1 - s), (1, s)):
+                sender = (v < j) if stream == 0 else (v > j)
+                for c in range(CHUNKS):
+                    pl.when(sender)(lambda: hop(stream, j, c).wait_send())
+
+    return step, finish, drain
+
+
+def times_rotation(left, rot, block, acc, rows):
     shard = left.shape[1]
 
     def body(i, carry):
         cols = pl.ds(pl.multiple_of(i * TILE, TILE), TILE)
-        rows = pl.ds(pl.multiple_of(block * shard, shard), shard)
-        acc[:, cols] += jnp.dot(left, rot[rows, cols], preferred_element_type=F32)
+        depth = pl.ds(pl.multiple_of(block * shard, shard), shard)
+        acc[rows, cols] += jnp.dot(left, rot[depth, cols], preferred_element_type=F32)
         return carry
 
     lax.fori_loop(0, acc.shape[1] // TILE, body, 0)
@@ -184,16 +190,19 @@
     index,
     logits,
     rot_hbm,
-    weighted,
-    diff_full,
+    weighted_all,
+    diff_all,
     inter_full,
     inter_own,
     rot,
     pool,
+    diff_full,
+    weighted,
     part,
     sums,
     acc,
     rot_sem,
+    own_sem,
     pool_s,
     pool_r,
     gd_s,
@@ -202,6 +211,10 @@
     red_r,
     gi_s,
     gi_r,
+    di_s,
+    di_r,
+    we_s,
+    we_r,
 ):
     me = lax.axis_index("mp")
     dp = lax.axis_index("dp")
@@ -218,52 +231,114 @@
     two = across(1, src, (1, near))
     one.start()
     two.start()
-    pool[0] = src[...]
+    owner = index[...]
+    lane = lax.broadcasted_iota(jnp.int32, (tokens, tokens), 1)
+
+    def pick(rows_in, who):
+        hit = (owner == lane + who * tokens).astype(F32).astype(BF)
+        return jnp.dot(hit, rows_in, preferred_element_type=F32)
+
+    acc[...] = pick(src[...], dp)
+    two.wait_recv()
+    acc[...] += pick(pool[1], near)
     one.wait_recv()
     three = across(2, pool.at[2], (3, near))
     three.start()
-    owner = index[...]
-    lane = lax.broadcasted_iota(jnp.int32, (tokens, tokens), 1)
-
-    def pick(slot, who):
-        hit = (owner == lane + who * tokens).astype(F32).astype(BF)
-        return jnp.dot(hit, pool[slot], preferred_element_type=F32)
-
-    acc[...] = pick(0, dp) + pick(2, far)
-    two.wait_recv()
-    acc[...] += pick(1, near)
+    acc[...] += pick(pool[2], far)
     three.wait_recv()
-    acc[...] += pick(3, both)
+    acc[...] += pick(pool[3], both)
     diff_full[me] = (acc[...] - base[...].astype(F32)).astype(BF)
     acc[...] = jnp.zeros_like(acc)
 
-    first = [True]
-
-    def use(j):
-        if first[0]:
-            first[0] = False
+    waited = []
+
+    def use(c, j):
+        if not waited:
+            waited.append(True)
             load.wait()
-        times_rotation(diff_full[j], rot, j, acc)
-
-    line_gather(diff_full, gd_s, gd_r, me, n, tokens, use)
-    weighted[...] = (jax.nn.sigmoid(logits[...]) * acc[...]).astype(BF)
-
-    def back(i, carry):
-        per = width // TILE
-        rows = pl.ds(pl.multiple_of(i * TILE, TILE), TILE)
-        cols = pl.ds(pl.multiple_of((i % per) * TILE, TILE), TILE)
-        part[i // per, :, cols] = contract_last(weighted[...], rot[rows, :]).astype(BF)
-        return carry
-
-    lax.fori_loop(0, rot.shape[0] // TILE, back, 0)
-    line_reduce(part, sums, red_s, red_r, acc, me, n, tokens)
-    mine = (base[...].astype(F32) + acc[...]).astype(BF)
-    inter_full[me] = mine
-    inter_own[...] = mine
-    line_gather(inter_full, gi_s, gi_r, me, n, tokens, lambda j: None)
-    one.wait_send()
-    two.wait_send()
-    three.wait_send()
+        rows = rows_of(c, tokens)
+        times_rotation(diff_full[j, rows], rot, j, acc, rows)
+
+    def prepare(c, j):
+        rows = rows_of(c, tokens)
+
+        def body(i, carry):
+            cols = pl.ds(pl.multiple_of(i * TILE, TILE), TILE)
+            depth = pl.ds(pl.multiple_of(j * width + i * TILE, TILE), TILE)
+            part[j, rows, cols] = contract_last(weighted[rows], rot[depth, :]).astype(BF)
+            return carry
+
+        lax.fori_loop(0, width // TILE, body, 0)
+
+    mask = jax.nn.sigmoid(logits[...])
+    copies = []
+    locals_ = []
+
+    def weigh(c):
+        rows = rows_of(c, tokens)
+        weighted[rows] = (mask * acc[rows]).astype(BF)
+
+    def exchange(c):
+        rows = rows_of(c, tokens)
+        for r in (2, 3, 1):
+            to = partner(dp, r)
+            copies.append(
+                send(diff_full.at[to, rows], diff_all.at[r, rows], di_s.at[r, c], di_r.at[r, c], "dp", to)
+            )
+            copies.append(
+                send(weighted.at[rows], weighted_all.at[r, rows], we_s.at[r, c], we_r.at[r, c], "dp", to)
+            )
+            copies[-2].start()
+            copies[-1].start()
+        mine = pltpu.make_async_copy(diff_full.at[dp, rows], diff_all.at[0, rows], own_sem.at[0, c])
+        ours = pltpu.make_async_copy(weighted.at[rows], weighted_all.at[0, rows], own_sem.at[1, c])
+        mine.start()
+        ours.start()
+        locals_.extend((mine, ours))
+
+    gather, gather_drain = line_gather(diff_full, gd_s, gd_r, me, n, tokens, use)
+    reduce, finish, reduce_drain = line_reduce(
+        part, sums, red_s, red_r, acc, me, n, tokens, prepare
+    )
+    spread, spread_drain = line_gather(inter_full, gi_s, gi_r, me, n, tokens, lambda c, j: None)
+
+    def settle(c):
+        finish(c)
+        rows = rows_of(c, tokens)
+        mine = (base[rows].astype(F32) + acc[rows]).astype(BF)
+        inter_full[me, rows] = mine
+        inter_own[rows] = mine
+
+    for k in range(n - 1):
+        gather(0, k)
+    gather(1, 0)
+    gather(0, n - 1)
+    weigh(0)
+    for s in range(n - 1):
+        reduce(0, s)
+        if s == 0:
+            exchange(0)
+        gather(1, s + 1)
+    settle(0)
+    spread(0, 0)
+    weigh(1)
+    for s in range(n - 1):
+        reduce(1, s)
+        if s == 0:
+            exchange(1)
+        spread(0, s + 1)
+    settle(1)
+    for k in range(n):
+        spread(1, k)
+    for copy in copies:
+        copy.wait_recv()
+    for copy in locals_:
+        copy.wait()
+    for copy in copies + [one, two, three]:
+        copy.wait_send()
+    gather_drain()
+    reduce_drain()
+    spread_drain()
 
 
 def recip_of(inter, n):
@@ -302,6 +377,10 @@
     def _():
         for j in range(n):
             out[j] = total[:, pl.ds(j * width, width)].astype(BF)
+
+
+def slot_of(a, b):
+    return (a + b) % 2 + 2 * ((a // 2 + b // 2) % 2)
 
 
 def back_kernel(
@@ -316,79 +395,154 @@
     rot,
     sums,
     dn,
+    dn_all,
+    inter_all,
     dinter,
     acc,
     stat,
+    recip,
+    aux,
     rot_sem,
     red_s,
     red_r,
     ga_s,
     ga_r,
-    ex_s,
-    ex_r,
+    in_s,
+    in_r,
+    dn_s,
+    dn_r,
+    au_s,
+    au_r,
     co_s,
     co_r,
 ):
     me = lax.axis_index("mp")
     dp = lax.axis_index("dp")
     tokens, width = part.shape[1:]
+    near, far = partner(dp, 1), partner(dp, 2)
     load = pltpu.make_async_copy(rot_hbm, rot, rot_sem)
     load.start()
     greet(me, n, dp)
-    line_reduce(part, sums, red_s, red_r, acc, me, n, tokens)
-    dn[me] = acc[...].astype(BF)
+
+    def use(c, j):
+        rows = rows_of(c, tokens)
+
+        @pl.when(j != dp)
+        def _():
+            r = slot_of(j, dp)
+            send(dn.at[j, rows], dn_all.at[r, rows], dn_s.at[r, c], dn_r.at[r, c], "dp", j).start()
+
+        scaled = gain[j].astype(F32) * dn[j, rows].astype(F32)
+        stat[rows] += jnp.sum(scaled * inter[j, rows].astype(F32), axis=1, keepdims=True)
+
+    reduce, finish, reduce_drain = line_reduce(part, sums, red_s, red_r, acc, me, n, tokens, None)
+    gather, gather_drain = line_gather(dn, ga_s, ga_r, me, n, tokens, use)
+
+    def settle(c):
+        finish(c)
+        rows = rows_of(c, tokens)
+        dn[me, rows] = acc[rows].astype(BF)
+
+    inters, auxes, ones, twos, threes = [], [], [], [], []
+
+    def couple(c):
+        rows = rows_of(c, tokens)
+        scale = recip[rows]
+        coef = scale * scale * scale * stat[rows] / (n * width)
+        lane = lax.broadcasted_iota(jnp.int32, (tokens // CHUNKS, 128), 1)
+        aux[0, rows] = jnp.where(lane < 64, scale, coef)
+        for r in (2, 3, 1):
+            copy = send(
+                aux.at[0, rows], aux.at[r, rows], au_s.at[r, c], au_r.at[r, c], "dp", partner(dp, r)
+            )
+            copy.start()
+            auxes.append(copy)
+        for j in range(n):
+            scaled = gain[j].astype(F32) * dn[j, rows].astype(F32)
+            dinter[j, rows] = (scale * scaled - inter[j, rows].astype(F32) * coef).astype(BF)
+        acc[rows] = jnp.zeros((tokens // CHUNKS, width), F32)
+        for j in range(n):
+            times_rotation(dinter[j, rows], rot, j, acc, rows)
+        coupled_all[0, rows] = (jax.nn.sigmoid(logits[...]) * acc[rows]).astype(BF)
+        own = coupled_all.at[0, rows]
+        one = send(own, coupled_all.at[2, rows], co_s.at[0, c], co_r.at[0, c], "dp", far)
+        two = send(own, coupled_all.at[1, rows], co_s.at[1, c], co_r.at[1, c], "dp", near)
+        one.start()
+        two.start()
+        ones.append(one)
+        twos.append(two)
+
+    def relay(c):
+        rows = rows_of(c, tokens)
+        ones[c].wait_recv()
+        three = send(
+            coupled_all.at[2, rows], coupled_all.at[3, rows], co_s.at[2, c], co_r.at[2, c], "dp", near
+        )
+        three.start()
+        threes.append(three)
+
+    def rebuild(c):
+        rows = rows_of(c, tokens)
+        scale_here = gain[dp].astype(F32)
+        dinter_all[0, rows] = dinter[dp, rows]
+        for i, r in enumerate((2, 3, 1)):
+            auxes[3 * c + i].wait_recv()
+            view = dn_all.at[r, rows]
+            send(view, view, dn_s.at[r, c], dn_r.at[r, c], "dp", partner(dp, r)).wait_recv()
+            scaled = scale_here * dn_all[r, rows].astype(F32)
+            scale, coef = aux[r, rows, 0:1], aux[r, rows, 64:65]
+            dinter_all[r, rows] = (
+                scale * scaled - inter_all[r, rows].astype(F32) * coef
+            ).astype(BF)
+
     stat[...] = jnp.zeros_like(stat)
-
-    def use(j):
-        scaled = gain[j].astype(F32) * dn[j].astype(F32)
-        stat[...] += jnp.sum(scaled * inter[j].astype(F32), axis=1, keepdims=True)
-
-    line_gather(dn, ga_s, ga_r, me, n, tokens, use)
-    recip = recip_of(inter, n)
-    coef = recip * recip * recip * stat[...] / (n * width)
-
-    copies = []
-    for j in range(n):
-        scaled = gain[j].astype(F32) * dn[j].astype(F32)
-        dinter[j] = (recip * scaled - inter[j].astype(F32) * coef).astype(BF)
-    for r in (2, 3, 1):
-        to = partner(dp, r)
-        copy = send(dinter.at[to], dinter_all.at[r], ex_s.at[r], ex_r.at[r], "dp", to)
-        copy.start()
-        copies.append(copy)
-    dinter_all[0] = dinter[dp]
+    for s in range(n - 1):
+        reduce(0, s)
+        if s == 0:
+            for r in (2, 3, 1):
+                to = partner(dp, r)
+                copy = send(inter.at[to], inter_all.at[r], in_s.at[r], in_r.at[r], "dp", to)
+                copy.start()
+                inters.append(copy)
+            recip[...] = recip_of(inter, n)
+    reduce(1, 0)
+    settle(0)
+    for k in range(n - 1):
+        gather(0, k)
+        if k + 1 < n - 1:
+            reduce(1, k + 1)
+    settle(1)
+    gather(1, 0)
+    gather(0, n - 1)
+    gather(1, 1)
     load.wait()
-    acc[...] = jnp.zeros_like(acc)
-    for j in range(n):
-        times_rotation(dinter[j], rot, j, acc)
-    coupled_all[0] = (jax.nn.sigmoid(logits[...]) * acc[...]).astype(BF)
-    near, far = partner(dp, 1), partner(dp, 2)
-    own = coupled_all.at[0]
-    one = send(own, coupled_all.at[2], co_s.at[0], co_r.at[0], "dp", far)
-    two = send(own, coupled_all.at[1], co_s.at[1], co_r.at[1], "dp", near)
-    one.start()
-    two.start()
-    one.wait_recv()
-    three = send(coupled_all.at[2], coupled_all.at[3], co_s.at[2], co_r.at[2], "dp", near)
-    three.start()
-    for copy in copies:
+    couple(0)
+    for k in range(2, n):
+        gather(1, k)
+    couple(1)
+    relay(0)
+    for copy in inters:
         copy.wait_recv()
-    two.wait_recv()
-    three.wait_recv()
-    for copy in copies + [one, two, three]:
+    rebuild(0)
+    relay(1)
+    rebuild(1)
+    for copy in twos + threes:
+        copy.wait_recv()
+    for copy in inters + auxes + ones + twos + threes:
         copy.wait_send()
-
-
-def grad_kernel(count, *refs):
-    dinter, coupled = refs[0], refs[1]
-    weighted = refs[2 : 2 + count]
-    diff = refs[2 + count : 2 + 2 * count]
-    out = refs[-1]
-    rows = pl.program_id(0)
+    for r in (1, 2, 3):
+        for c in range(CHUNKS):
+            view = dn_all.at[r, rows_of(c, tokens)]
+            send(view, view, dn_s.at[r, c], dn_r.at[r, c], "dp", partner(dp, r)).wait_send()
+    reduce_drain()
+    gather_drain()
+
+
+def grad_kernel(count, dinter, coupled, weighted, diff, out):
     acc = jnp.zeros(out.shape, F32)
     for r in range(count):
-        acc = acc + contract_first(dinter[r], weighted[r][...])
-        acc = acc + contract_first(diff[r][...], coupled[r])
+        acc = acc + contract_first(dinter[r], weighted[r])
+        acc = acc + contract_first(diff[r], coupled[r])
     out[...] = acc
 
 
@@ -426,18 +580,22 @@
     whole = jax.ShapeDtypeStruct((n, tokens, width), BF)
     one = jax.ShapeDtypeStruct((tokens, width), BF)
     line = (2, n - 1, CHUNKS)
-    weighted, diff_full, inter_full, interchanged = pl.pallas_call(
+    spread = jax.ShapeDtypeStruct((peers, tokens, width), BF)
+    weighted_all, diff_all, inter_full, interchanged = pl.pallas_call(
         functools.partial(front_kernel, n),
-        out_shape=(one, whole, whole, one),
+        out_shape=(spread, spread, whole, one),
         in_specs=[vmem()] * 4 + [anywhere()],
-        out_specs=(vmem(),) * 4,
+        out_specs=(anywhere(), anywhere(), vmem(), vmem()),
         scratch_shapes=[
             pltpu.VMEM((full, width), BF),
             pltpu.VMEM((peers, tokens, width), BF),
             pltpu.VMEM((n, tokens, width), BF),
+            pltpu.VMEM((tokens, width), BF),
+            pltpu.VMEM((n, tokens, width), BF),
             pltpu.VMEM((2, n, tokens, width), BF),
             pltpu.VMEM((tokens, width), F32),
             pltpu.SemaphoreType.DMA,
+            dma(2, CHUNKS),
             dma(3),
             dma(3),
             dma(*line),
@@ -446,18 +604,14 @@
             dma(2, n, CHUNKS),
             dma(*line),
             dma(*line),
+            dma(peers, CHUNKS),
+            dma(peers, CHUNKS),
+            dma(peers, CHUNKS),
+            dma(peers, CHUNKS),
         ],
         compiler_params=pltpu.CompilerParams(collective_id=0, has_side_effects=True),
         name="front",
     )(source_states, base_states, index, logits, rotation)
-
-    dp = lax.axis_index("dp")
-    weights_of = [weighted]
-    diffs_of = [diff_full[dp]]
-    for r in range(1, peers):
-        perm = [(i, i ^ r) for i in range(peers)]
-        weights_of.append(lax.ppermute(weighted, "dp", perm))
-        diffs_of.append(lax.ppermute(diff_full[dp ^ r], "dp", perm))
 
     block = 512 if hidden % 512 == 0 else hidden
     part = pl.pallas_call(
@@ -490,9 +644,13 @@
             pltpu.VMEM((full, width), BF),
             pltpu.VMEM((2, n, tokens, width), BF),
             pltpu.VMEM((n, tokens, width), BF),
+            pltpu.VMEM((peers, tokens, width), BF),
+            pltpu.VMEM((peers, tokens, width), BF),
             pltpu.VMEM((n, tokens, width), BF),
             pltpu.VMEM((tokens, width), F32),
             pltpu.VMEM((tokens, 1), F32),
+            pltpu.VMEM((tokens, 1), F32),
+            pltpu.VMEM((peers, tokens, 128), F32),
             pltpu.SemaphoreType.DMA,
             dma(2, n, CHUNKS),
             dma(2, n, CHUNKS),
@@ -500,8 +658,12 @@
             dma(*line),
             dma(peers),
             dma(peers),
-            dma(3),
-            dma(3),
+            dma(peers, CHUNKS),
+            dma(peers, CHUNKS),
+            dma(peers, CHUNKS),
+            dma(peers, CHUNKS),
+            dma(3, CHUNKS),
+            dma(3, CHUNKS),
         ],
         compiler_params=pltpu.CompilerParams(collective_id=1, has_side_effects=True),
         name="back",
@@ -515,12 +677,12 @@
         in_specs=[
             pl.BlockSpec((peers, tokens, rows), lambda i: (0, 0, i)),
             pl.BlockSpec((peers, tokens, width), lambda i: (0, 0, 0)),
-        ]
-        + [pl.BlockSpec((tokens, width), lambda i: (0, 0))] * peers
-        + [pl.BlockSpec((tokens, rows), lambda i: (0, i))] * peers,
+            pl.BlockSpec((peers, tokens, width), lambda i: (0, 0, 0)),
+            pl.BlockSpec((peers, tokens, rows), lambda i: (0, 0, i)),
+        ],
         out_specs=pl.BlockSpec((rows, width), lambda i: (i, 0)),
         name="grad",
-    )(dinter_all, coupled_all, *weights_of, *diffs_of)
+    )(dinter_all, coupled_all, weighted_all, diff_all)
     return (rotation_grad, interchanged)
 
 
@@ -590,7 +752,7 @@
         fits = (
             width % TILE == 0
             and mesh.shape["dp"] == 4
-            and 1 < n <= 8
+            and n == 4
             and n * width == full
             and full // 4 == width
             and tokens % (16 * CHUNKS) == 0

time: 230 us -> 212 us (0.922)
  Pallas kernels: 213 us -> 205 us
  waiting for transfers between devices: 5.62 us -> 0 us
  starting transfers between devices: 3.78 us -> 0 us
    pallas_call x1, Pallas kernels: 75 us -> 63.3 us  [fast(): pl.pallas_call(functools.partial(back_kernel, n), out_shape=(jax.ShapeDty...]
    ppermute x6 -> x0, waiting for transfers between devices: 5.62 us -> none  [the longest x3 5.62 us: fast(): diffs_of.append(lax.ppermute(diff_full[dp ^ r], 'dp', perm))]
    ppermute x6 -> x0, starting transfers between devices: 3.78 us -> none  [the longest x3 2.86 us: fast(): weights_of.append(lax.ppermute(weighted, 'dp', perm))]
    pallas_call x1, Pallas kernels: 92.3 us -> 96.1 us  [fast(): pl.pallas_call(functools.partial(front_kernel, n), out_shape=(spread, spr...]
  transfers between devices with their start and end apart: 6 -> 0, of which waited for: 1 -> 0; matrix products, arithmetic and copies ran while one was open for 1% -> 0% of each run, Pallas kernels for 49% -> 0%
where the time goes in v2:
time: 212 us; the launch traced here: 211 us
  Pallas kernels  205 us (97%)
  local copies, waits for them, and re-layouts  4.09 us (2%)
    pallas_call x1, Pallas kernels, fast(): pl.pallas_call(functools.partial(front_kernel, n), out_shape=(spread, spr...  96.1 us
    pallas_call x1, Pallas kernels, fast(): pl.pallas_call(functools.partial(back_kernel, n), out_shape=(jax.ShapeDty...  63.3 us
    pallas_call x1, Pallas kernels, fast(): pl.pallas_call(functools.partial(ffn_kernel, n), out_shape=whole, grid=(h...  37.4 us
    pallas_call x1, Pallas kernels, fast(): pl.pallas_call(functools.partial(grad_kernel, peers), out_shape=jax.Shape...  8.29 us

profile of v2, /device:TPU:0, one launch (start us, length us, event | category | flops | bytes accessed | tf_op | source)
XLA Modules:
  0.0 210.6 jit_solution(15998851938615525423)
XLA Ops:
  0.6 0.7 multiply_add_fusion
  1.3 1.3 reshape.8.gain
  2.6 1.3 broadcast_in_dim.11.gain
  3.9 0.8 copy.18.index
  4.7 96.1 %front.1 = (bf16[4,160,1024]{2,1,0:T(8,128)(2,1)}, bf16[4,160,1024]{2,1,0:T(8,128)(2,1)}, bf16[4,160,1024]{2,1,0:T(8,128)(2,1)}, bf16[160,1024]{1,0:T(8,128)(2,1)}) custom-call(bf16[160,1024]{1,0:T(8,128)(2,1)} %src.1, bf16[160,1024]{1,0:T(8,128)(2,1)} %base.1, s32[160,1]{1,0:T(8,128)} %copy.18.index, f32[1,1024]{1,0:T(1,128)} %bitcast.2, ...), custom_call_target="tpu_custom_call" | custom-call | tf_op jit(solution)/shard_map/front/pallas_call | solution.py:584
  100.8 37.4 %ffn.1.part = bf16[4,160,1024]{2,1,0:T(8,128)(2,1)} custom-call(bf16[4,160,1024]{2,1,0:T(8,128)(2,1)} %get-tuple-element.8.inter, bf16[1,4096]{1,0:T(2,128)(2,1)} %broadcast_in_dim.11.gain, bf16[4096,3584]{1,0:T(8,128)(2,1)} %wg.1, bf16[4096,3584]{1,0:T(8,128)(2,1)} %wu.1, bf16[160,3584]{1,0:T(8,128)(2,1)} %cot.1), custom_call_target="tpu_custom_call" | custom-call | flops 18790481920 | bytes 58720256 | tf_op jit(solution)/shard_map/ffn/pallas_call | solution.py:617
  138.2 63.3 %back.1 = (bf16[4,160,1024]{2,1,0:T(8,128)(2,1)}, bf16[4,160,1024]{2,1,0:T(8,128)(2,1)}) custom-call(bf16[4,160,1024]{2,1,0:T(8,128)(2,1)} %ffn.1.part, bf16[4,160,1024]{2,1,0:T(8,128)(2,1)} %get-tuple-element.8.inter, bf16[4,1,1024]{2,1,0:T(2,128)(2,1)} %reshape.8.gain, f32[1,1024]{1,0:T(1,128)} %bitcast.3, bf16[4096,1024]{1,0:T(8,128)(2,1)} %rot_hbm.3), custom_call_target="tpu_custom_call" | custom-call | tf_op jit(solution)/shard_map/back/pallas_call | solution.py:638
  201.6 0.0 copy-start
  201.6 8.3 %grad.1 = f32[1024,1024]{1,0:T(8,128)} custom-call(bf16[4,160,1024]{2,1,0:T(8,128)(2,1)} %get-tuple-element.9.dinter, bf16[4,160,1024]{2,1,0:T(8,128)(2,1)} %get-tuple-element.10.coupled, bf16[4,160,1024]{2,1,0:T(8,128)(2,1)} %get-tuple-element.11.weighted, bf16[4,160,1024]{2,1,0:T(8,128)(2,1)} %get-tuple-element.12.diff), custom_call_target="tpu_custom_call" | custom-call | tf_op jit(solution)/shard_map/grad/pallas_call | solution.py:673
  209.9 0.0 copy-done
  209.9 0.7 copy.21
Async XLA Ops:
  201.6 8.3 %copy-start = (bf16[160,1024]{1,0:T(8,128)(2,1)S(1)}, bf16[160,1024]{1,0:T(8,128)(2,1)}, u32[]{:S(2)}) copy-start(bf16[160,1024]{1,0:T(8,128)(2,1)} %get-tuple-element.17) | copy-start | bytes 983044

commit v3 on v2

--- a/solution.py
+++ b/solution.py
@@ -350,33 +350,23 @@
     return lax.rsqrt(square / (n * width) + 1e-05)
 
 
-def ffn_kernel(n, inter, gain, wg, wu, cot, out, normed, total):
+def ffn_kernel(n, inter, gain, wg, wu, cot, dgate, dup, normed):
     tokens, width = inter.shape[1:]
-    step = pl.program_id(0)
-
-    @pl.when(step == 0)
+
+    @pl.when(pl.program_id(0) == 0)
     def _():
         recip = recip_of(inter, n)
         for j in range(n):
             cols = pl.ds(j * width, width)
             scale = gain[:, cols].astype(F32)
             normed[:, cols] = (inter[j].astype(F32) * recip * scale).astype(BF)
-        total[...] = jnp.zeros_like(total)
 
     gate = jnp.dot(normed[...], wg[...], preferred_element_type=F32)
     up = jnp.dot(normed[...], wu[...], preferred_element_type=F32)
     sig = jax.nn.sigmoid(gate)
     cotan = cot[...].astype(F32)
-    dgate = (cotan * up * sig * (1.0 + gate * (1.0 - sig))).astype(BF)
-    dup = (cotan * gate * sig).astype(BF)
-    for i in range(n * width // 512):
-        rows = pl.ds(i * 512, 512)
-        total[:, rows] += contract_last(dgate, wg[rows, :]) + contract_last(dup, wu[rows, :])
-
-    @pl.when(step == pl.num_programs(0) - 1)
-    def _():
-        for j in range(n):
-            out[j] = total[:, pl.ds(j * width, width)].astype(BF)
+    dgate[...] = (cotan * up * sig * (1.0 + gate * (1.0 - sig))).astype(BF)
+    dup[...] = (cotan * gate * sig).astype(BF)
 
 
 def slot_of(a, b):
@@ -385,14 +375,19 @@
 
 def back_kernel(
     n,
-    part,
+    dgate,
+    dup,
     inter,
     gain,
     logits,
     rot_hbm,
+    wg,
+    wu,
     dinter_all,
     coupled_all,
     rot,
+    part,
+    blocks,
     sums,
     dn,
     dn_all,
@@ -403,6 +398,7 @@
     recip,
     aux,
     rot_sem,
+    block_sem,
     red_s,
     red_r,
     ga_s,
@@ -418,11 +414,61 @@
 ):
     me = lax.axis_index("mp")
     dp = lax.axis_index("dp")
-    tokens, width = part.shape[1:]
+    tokens, width = inter.shape[1:]
     near, far = partner(dp, 1), partner(dp, 2)
     load = pltpu.make_async_copy(rot_hbm, rot, rot_sem)
-    load.start()
+    size = blocks.shape[2]
+    per = width // size
+
+    def fetch(row, slot):
+        rows = pl.ds(pl.multiple_of(row, size), size)
+        return (
+            pltpu.make_async_copy(wg.at[rows, :], blocks.at[slot, 0], block_sem.at[slot, 0]),
+            pltpu.make_async_copy(wu.at[rows, :], blocks.at[slot, 1], block_sem.at[slot, 1]),
+        )
+
+    flip = (me * 2) // n
+    order = []
+    for s in range(n // 2):
+        for j in (n - 1 - s, s):
+            order.append(j + flip * (n - 1 - 2 * j))
+    for copy in fetch(order[0] * width, 0):
+        copy.start()
     greet(me, n, dp)
+    done = []
+
+    def prepare(c, j):
+        if c > 0:
+            return
+        p = len(done)
+        done.append(p)
+        here = order[p]
+        after = order[p + 1] if p + 1 < n else None
+
+        def body(i, carry):
+            slot = i % 2
+            if after is not None:
+                end = (i + 1) // per
+                row = (here * width + (i + 1) * size) * (1 - end) + after * width * end
+                for copy in fetch(row, 1 - slot):
+                    copy.start()
+            else:
+
+                @pl.when(i + 1 < per)
+                def _():
+                    for copy in fetch(here * width + (i + 1) * size, 1 - slot):
+                        copy.start()
+
+            for copy in fetch(here * width + i * size, slot):
+                copy.wait()
+            cols = pl.ds(pl.multiple_of(i * size, size), size)
+            part[here, :, cols] = (
+                contract_last(dgate[...], blocks[slot, 0])
+                + contract_last(dup[...], blocks[slot, 1])
+            ).astype(BF)
+            return carry
+
+        lax.fori_loop(0, per, body, 0)
 
     def use(c, j):
         rows = rows_of(c, tokens)
@@ -435,7 +481,7 @@
         scaled = gain[j].astype(F32) * dn[j, rows].astype(F32)
         stat[rows] += jnp.sum(scaled * inter[j, rows].astype(F32), axis=1, keepdims=True)
 
-    reduce, finish, reduce_drain = line_reduce(part, sums, red_s, red_r, acc, me, n, tokens, None)
+    reduce, finish, reduce_drain = line_reduce(part, sums, red_s, red_r, acc, me, n, tokens, prepare)
     gather, gather_drain = line_gather(dn, ga_s, ga_r, me, n, tokens, use)
 
     def settle(c):
@@ -505,6 +551,7 @@
                 copy.start()
                 inters.append(copy)
             recip[...] = recip_of(inter, n)
+    load.start()
     reduce(1, 0)
     settle(0)
     for k in range(n - 1):
@@ -614,9 +661,9 @@
     )(source_states, base_states, index, logits, rotation)
 
     block = 512 if hidden % 512 == 0 else hidden
-    part = pl.pallas_call(
+    dgate, dup = pl.pallas_call(
         functools.partial(ffn_kernel, n),
-        out_shape=whole,
+        out_shape=(jax.ShapeDtypeStruct((tokens, hidden), BF),) * 2,
         grid=(hidden // block,),
         in_specs=[
             pl.BlockSpec((n, tokens, width), lambda i: (0, 0, 0)),
@@ -625,23 +672,20 @@
             pl.BlockSpec((full, block), lambda i: (0, i)),
             pl.BlockSpec((tokens, block), lambda i: (0, i)),
         ],
-        out_specs=pl.BlockSpec((n, tokens, width), lambda i: (0, 0, 0)),
-        scratch_shapes=[pltpu.VMEM((tokens, full), BF), pltpu.VMEM((tokens, full), F32)],
-        cost_estimate=pl.CostEstimate(
-            flops=8 * tokens * full * hidden,
-            bytes_accessed=4 * full * hidden,
-            transcendentals=tokens * hidden,
-        ),
+        out_specs=(pl.BlockSpec((tokens, block), lambda i: (0, i)),) * 2,
+        scratch_shapes=[pltpu.VMEM((tokens, full), BF)],
         name="ffn",
     )(inter_full, norm_gain[None, :], gate_weight, up_weight, hidden_cot)
 
     dinter_all, coupled_all = pl.pallas_call(
         functools.partial(back_kernel, n),
         out_shape=(jax.ShapeDtypeStruct((peers, tokens, width), BF),) * 2,
-        in_specs=[vmem()] * 4 + [anywhere()],
+        in_specs=[vmem()] * 5 + [anywhere()] * 3,
         out_specs=(vmem(),) * 2,
         scratch_shapes=[
             pltpu.VMEM((full, width), BF),
+            pltpu.VMEM((n, tokens, width), BF),
+            pltpu.VMEM((2, 2, 256, hidden), BF),
             pltpu.VMEM((2, n, tokens, width), BF),
             pltpu.VMEM((n, tokens, width), BF),
             pltpu.VMEM((peers, tokens, width), BF),
@@ -652,6 +696,7 @@
             pltpu.VMEM((tokens, 1), F32),
             pltpu.VMEM((peers, tokens, 128), F32),
             pltpu.SemaphoreType.DMA,
+            dma(2, 2),
             dma(2, n, CHUNKS),
             dma(2, n, CHUNKS),
             dma(*line),
@@ -667,7 +712,16 @@
         ],
         compiler_params=pltpu.CompilerParams(collective_id=1, has_side_effects=True),
         name="back",
-    )(part, inter_full, norm_gain.reshape(n, 1, width), logits, rotation)
+    )(
+        dgate,
+        dup,
+        inter_full,
+        norm_gain.reshape(n, 1, width),
+        logits,
+        rotation,
+        gate_weight,
+        up_weight,
+    )
 
     rows = 256
     rotation_grad = pl.pallas_call(

time: 212 us -> 220 us (1.038)
  Pallas kernels: 205 us -> 213 us
    pallas_call x1, Pallas kernels: 63.3 us -> 85.1 us  [fast(): pl.pallas_call(functools.partial(back_kernel, n), out_shape=(jax.ShapeDty...]
    pallas_call x1, Pallas kernels: 37.4 us -> 24 us  [fast(): pl.pallas_call(functools.partial(ffn_kernel, n), out_shape=(jax.ShapeDtyp...]
where the time goes in v3:
time: 220 us; the launch traced here: 219 us
  Pallas kernels  213 us (97%)
  local copies, waits for them, and re-layouts  4.09 us (2%)
    pallas_call x1, Pallas kernels, fast(): pl.pallas_call(functools.partial(front_kernel, n), out_shape=(spread, spr...  95.9 us
    pallas_call x1, Pallas kernels, fast(): pl.pallas_call(functools.partial(back_kernel, n), out_shape=(jax.ShapeDty...  85.1 us
    pallas_call x1, Pallas kernels, fast(): pl.pallas_call(functools.partial(ffn_kernel, n), out_shape=(jax.ShapeDtyp...  24 us
    pallas_call x1, Pallas kernels, fast(): pl.pallas_call(functools.partial(grad_kernel, peers), out_shape=jax.Shape...  8.29 us

profile of v3, /device:TPU:0, one launch (start us, length us, event | category | flops | bytes accessed | tf_op | source)
XLA Modules:
  0.0 218.7 jit_solution(1564165704078101755)
XLA Ops:
  0.6 0.7 multiply_add_fusion
  1.3 1.3 reshape.8.gain
  2.6 1.3 broadcast_in_dim.11.gain
  3.9 0.8 copy.18.index
  4.7 95.9 %front.1 = (bf16[4,160,1024]{2,1,0:T(8,128)(2,1)}, bf16[4,160,1024]{2,1,0:T(8,128)(2,1)}, bf16[4,160,1024]{2,1,0:T(8,128)(2,1)}, bf16[160,1024]{1,0:T(8,128)(2,1)}) custom-call(bf16[160,1024]{1,0:T(8,128)(2,1)} %src.1, bf16[160,1024]{1,0:T(8,128)(2,1)} %base.1, s32[160,1]{1,0:T(8,128)} %copy.18.index, f32[1,1024]{1,0:T(1,128)} %bitcast.2, ...), custom_call_target="tpu_custom_call" | custom-call | tf_op jit(solution)/shard_map/front/pallas_call | solution.py:631
  100.6 24.0 %ffn.1 = (bf16[160,3584]{1,0:T(8,128)(2,1)}, bf16[160,3584]{1,0:T(8,128)(2,1)}) custom-call(bf16[4,160,1024]{2,1,0:T(8,128)(2,1)} %get-tuple-element.10.inter, bf16[1,4096]{1,0:T(2,128)(2,1)} %broadcast_in_dim.11.gain, bf16[4096,3584]{1,0:T(8,128)(2,1)} %wg.3, bf16[4096,3584]{1,0:T(8,128)(2,1)} %wu.3, bf16[160,3584]{1,0:T(8,128)(2,1)} %cot.1), custom_call_target="tpu_custom_call" | custom-call | tf_op jit(solution)/shard_map/ffn/pallas_call | solution.py:664
  124.6 85.1 %back.1 = (bf16[4,160,1024]{2,1,0:T(8,128)(2,1)}, bf16[4,160,1024]{2,1,0:T(8,128)(2,1)}) custom-call(bf16[160,3584]{1,0:T(8,128)(2,1)} %get-tuple-element.11.dgate, bf16[160,3584]{1,0:T(8,128)(2,1)} %get-tuple-element.12.dup, bf16[4,160,1024]{2,1,0:T(8,128)(2,1)} %get-tuple-element.10.inter, bf16[4,1,1024]{2,1,0:T(2,128)(2,1)} %reshape.8.gain, ...), custom_call_target="tpu_custom_call" | custom-call | tf_op jit(solution)/shard_map/back/pallas_call | solution.py:680
  209.7 0.0 copy-start
  209.7 8.3 %grad.1 = f32[1024,1024]{1,0:T(8,128)} custom-call(bf16[4,160,1024]{2,1,0:T(8,128)(2,1)} %get-tuple-element.13.dinter, bf16[4,160,1024]{2,1,0:T(8,128)(2,1)} %get-tuple-element.14.coupled, bf16[4,160,1024]{2,1,0:T(8,128)(2,1)} %get-tuple-element.15.weighted, bf16[4,160,1024]{2,1,0:T(8,128)(2,1)} %get-tuple-element.16.diff), custom_call_target="tpu_custom_call" | custom-call | tf_op jit(solution)/shard_map/grad/pallas_call | solution.py:727
  218.0 0.0 copy-done
  218.0 0.7 copy.21
Async XLA Ops:
  209.7 8.3 %copy-start = (bf16[160,1024]{1,0:T(8,128)(2,1)S(1)}, bf16[160,1024]{1,0:T(8,128)(2,1)}, u32[]{:S(2)}) copy-start(bf16[160,1024]{1,0:T(8,128)(2,1)} %get-tuple-element.21) | copy-start | bytes 983044
